TPU v7x, 32 devices: a whole 2x2x4 slice. The times are simulated.
32 devices in a mesh: seg: 2 (over y), ch: 16 (over z, x, core).
Axes of the slice: x: 2, y: 2, z: 4, core: 2. Of those that a mesh axis runs over, the one named last changes fastest.
Arguments:
- strain: float32 [2, 1024, 2048], P('seg', 'ch')
- ref_local: int32 [4, 16], replicated, may hold values from 0 to 127, as said below
- owners: int32 [4], replicated, may hold values from 0 to 15, as said below
Outputs:
- toeplitz_blocks: float32 [64, 2048, 64], P('seg', 'ch')
Inputs may be any that keep to these rules, and one draw needn't show every extreme that they name: `ref_local`: each row holds 16 distinct offsets; the first row holds 127. `owners`: the 4 entries are distinct, and one of them is 15.
All inputs are finite; a program needn't handle non-finite values.
Results may differ from a plain program's by a relative error of at most 0.0029.
Values may be sent and summed in bfloat16 or wider, within the bound.
A program may use at most 64 MiB of HBM per device.

v0:
```python
import jax
import jax.numpy as jnp
from jax import lax
from jax.sharding import PartitionSpec as P

L = 64


def spread_2(block, axis, holder):
    block = jnp.where(lax.axis_index(axis) == holder, block, jnp.zeros_like(block))
    return lax.psum(block, axis)


def detrend_cols(series):
    n_total = series.shape[0]
    mid_time = (n_total - 1) / 2.0
    spread = n_total * (n_total * n_total - 1) / 12.0
    centred = (jnp.arange(n_total, dtype=jnp.float32) - mid_time)[:, None]
    level_val = jnp.sum(series, axis=0) / n_total
    slope_val = jnp.sum(centred * series, axis=0) / spread
    return (series - level_val - slope_val * centred).astype(jnp.bfloat16)


def owner_panels(detrended, ref_local, owners):
    pieces = []
    for panel_id in range(ref_local.shape[0]):
        own_cols = jnp.take(detrended, ref_local[panel_id], axis=1)
        pieces.append(spread_2(own_cols, "ch", owners[panel_id]))
    return jnp.concatenate(pieces, axis=1)


def per_device(strain, ref_local, owners):
    my_rows = strain[0]
    s_dev, chans = my_rows.shape
    n_ch = lax.axis_size("ch")
    n_seg = lax.axis_size("seg")
    n_total = s_dev * n_ch
    c_dev = chans // n_ch
    series = lax.all_to_all(my_rows, "ch", split_axis=1, concat_axis=0, tiled=True)
    detrended = detrend_cols(series)
    panels = owner_panels(detrended, ref_local, owners)
    width_ref = panels.shape[1]
    padded = jnp.concatenate([detrended, jnp.zeros((L, c_dev), jnp.bfloat16)], axis=0)
    blk_rows = min(512, n_total)
    n_blocks = n_total // blk_rows
    lag_dev = L // n_seg
    lag_count = lax.axis_size("seg") * lag_dev

    def add_block(blk_idx, running):
        blk_start = blk_idx * blk_rows
        window = lax.dynamic_slice_in_dim(padded, blk_start, blk_rows + lag_count - 1, 0)
        lagged = jnp.concatenate(
            [window[lag_off : lag_off + blk_rows] for lag_off in range(lag_count)], axis=1
        )
        ref_block = lax.dynamic_slice_in_dim(panels, blk_start, blk_rows, 0)
        return running + lax.dot_general(
            lagged, ref_block, (((0,), (0,)), ((), ())), preferred_element_type=jnp.float32
        )

    start_acc = jnp.zeros((lag_count * c_dev, width_ref), jnp.float32)
    running = lax.fori_loop(0, n_blocks, add_block, start_acc)
    summed = lax.psum_scatter(
        running.reshape(lag_count, c_dev, width_ref), "seg", scatter_dimension=0, tiled=True
    )
    lag_ids = (lax.axis_index("seg") * lag_dev + jnp.arange(lag_dev, dtype=jnp.int32)).astype(
        jnp.float32
    )
    return summed / (n_seg * (n_total - lag_ids))[:, None, None]


def solution(mesh):
    in_specs = (P("seg", "ch", None), P(), P())
    out_specs = P("seg", "ch", None)
    return jax.shard_map(
        per_device, mesh=mesh, in_specs=in_specs, out_specs=out_specs, check_vma=False
    )
```

profile of v0, /device:TPU:0, one launch (start us, length us, event | category | flops | bytes accessed | tf_op | source)
XLA Modules:
  0.0 272.1 jit_solution(4993539267196957720)
XLA Ops:
  6.5 1.1 copy.23
  7.7 1.0 copy.16
  8.6 7.4 %all-to-all-start = ((f32[64,16,128]{2,0,1:T(8,128)}), f32[64,16,128]{2,0,1:T(8,128)S(1)}, u32[]{:S(2)}, u32[]{:S(2)}) async-start(f32[64,16,128]{2,0,1:T(8,128)} %copy.16), calls=%async_computation | async-start | bytes 1048576 | tf_op jit(solution)/shard_map/all_to_all | solution.py:39
  16.1 1.5 fusion.3
  20.0 0.8 compare_and_fusion.3
  20.9 9.4 %all-to-all-done = f32[64,16,128]{2,0,1:T(8,128)S(1)} async-done(((f32[64,16,128]{2,0,1:T(8,128)}), f32[64,16,128]{2,0,1:T(8,128)S(1)}, u32[]{:S(2)}, u32[]{:S(2)}) %all-to-all-start) | async-done | bytes 524320 | tf_op jit(solution)/shard_map/all_to_all | solution.py:39
  36.4 88.2 %all-reduce.4.cloned.1.call-done = (bf16[1024,16]{0,1:T(8,128)(2,1)}, bf16[1024,16]{0,1:T(8,128)(2,1)}, bf16[1024,16]{0,1:T(8,128)(2,1)}, bf16[1024,16]{0,1:T(8,128)(2,1)}) async-done(((bf16[1024,16]{0,1:T(8,128)(2,1)}, bf16[1024,16]{0,1:T(8,128)(2,1)}, bf16[1024,16]{0,1:T(8,128)(2,1)}, bf16[1024,16]{0,1:T(8,128)(2,1)}), (bf16[1024,16]{0,1:T(8,128)(2,1)}, bf16[1024,16]{0,1:T(8,128)(2,1)}, ...) | async-done | bytes 131088 | tf_op jit(solution)/shard_map/psum | solution.py:11
  124.6 0.8 pad_maximum_fusion
  125.4 101.3 %while.14 = (s32[]{:T(128)}, f32[8192,64]{0,1:T(8,128)S(1)}, bf16[1088,128]{1,0:T(8,128)(2,1)S(1)}, bf16[1024,64]{0,1:T(8,128)(2,1)S(1)}, s32[]{:T(128)}, /*inde...) while((s32[]{:T(128)}, f32[8192,64]{0,1:T(8,128)S(1)}, ...), condition=%wide.region_7.9_spmd.clone, body=%wide.region_6.8_spmd.clone.sunk | while | flops 537919552 | bytes 29427356 | solution.py:61
  135.3 0.8 constant_dynamic-update-slice_fusion.142
  143.1 0.7 constant_dynamic-update-slice_fusion.153
  146.7 0.8 constant_dynamic-update-slice_fusion.158
  150.3 0.8 constant_dynamic-update-slice_fusion.163
  163.1 0.8 constant_dynamic-update-slice_fusion.181
  170.9 5.2 %convolution_add_fusion.2 = f32[8192,64]{0,1:T(8,128)S(1)} fusion(bf16[512,8192]{1,0:T(8,128)(2,1)} %constant_dynamic-update-slice_fusion.191, f32[8192,64]{0,1:T(8,128)S(1)} %get-tuple-element.251, pred[]{:T(512)S(6)} %compare.4, bf16[1024,64]{0,1:T(8,128)(2,1)S(1)} %get-tuple-element.325, s32[]{:T(128)S(6)} %select_n.98), kind=kOutput, calls=%fused_computation.4.clone.1 | convolution fusion | flops 537919488 | bytes 12648453 | tf_op jit(solution)/shard_map/while/body/eval_jaxpr/dot_general | solution.py:56
  185.9 0.8 constant_dynamic-update-slice_fusion.142
  197.3 0.8 constant_dynamic-update-slice_fusion.158
  200.9 0.8 constant_dynamic-update-slice_fusion.163
  213.7 0.8 constant_dynamic-update-slice_fusion.181
  221.5 5.2 %convolution_add_fusion.2 = f32[8192,64]{0,1:T(8,128)S(1)} fusion(bf16[512,8192]{1,0:T(8,128)(2,1)} %constant_dynamic-update-slice_fusion.191, f32[8192,64]{0,1:T(8,128)S(1)} %get-tuple-element.251, pred[]{:T(512)S(6)} %compare.4, bf16[1024,64]{0,1:T(8,128)(2,1)S(1)} %get-tuple-element.325, s32[]{:T(128)S(6)} %select_n.98), kind=kOutput, calls=%fused_computation.4.clone.1 | convolution fusion | flops 537919488 | bytes 12648453 | tf_op jit(solution)/shard_map/while/body/eval_jaxpr/dot_general | solution.py:56
  226.7 1.7 copy.24
  228.5 33.8 %reduce-scatter.2.cloned.1.call-done = f32[32,128,64]{1,0,2:T(8,128)} async-done(((f32[64,128,64]{1,0,2:T(8,128)}), f32[32,128,64]{1,0,2:T(8,128)}) %reduce-scatter.2.cloned.1.call-update) | async-done | bytes 1048592 | tf_op jit(solution)/shard_map/reduce_scatter | solution.py:62
  262.3 1.4 broadcast_divide_fusion
  263.7 1.6 copy.20
  (144 shorter events, 90.2 us)
Async XLA Ops:
  8.6 21.7 %all-to-all-start = ((f32[64,16,128]{2,0,1:T(8,128)}), f32[64,16,128]{2,0,1:T(8,128)S(1)}, u32[]{:S(2)}, u32[]{:S(2)}) async-start(f32[64,16,128]{2,0,1:T(8,128)} %copy.16), calls=%async_computation | async-start | bytes 1048576 | tf_op jit(solution)/shard_map/all_to_all | solution.py:39
  16.0 108.6 %all-reduce.4.cloned.1.call-start = ((), (), s32[]{:S(2)}) async-start(), calls=%async_computation.3 | async-start | bytes 262144 | tf_op jit(solution)/shard_map/psum | solution.py:11
  36.2 226.1 %reduce-scatter.2.cloned.1.call-start = ((), (), s32[]{:S(2)}) async-start(), calls=%async_computation.2 | async-start | bytes 3145728 | tf_op jit(solution)/shard_map/reduce_scatter | solution.py:62
Sparse Core Ops, SparseCore 0:
  36.3 88.2 all-reduce.3
  228.6 33.6 reduce-scatter.1
where the time goes:
time: 273 us; the launch traced here: 272 us
  waiting for transfers between devices  131 us (48%)
  local copies, waits for them, and re-layouts  100 us (37%)
  between operations  16 us (6%)
  matrix products  10.4 us (4%)
  starting transfers between devices  7.47 us (3%)
  other arithmetic  6.38 us (2%)
    while x126, local copies, waits for them, and re-layouts  89.4 us
    psum x1, waiting for transfers between devices, spread_2(): return lax.psum(block, axis)  88.2 us
    reduce_scatter x1, waiting for transfers between devices, per_device(): lax.psum_scatter(running.reshape(lag_count, c_dev, width_ref), 'seg', sca...  33.8 us
    dot_general x2, matrix products, add_block(): lax.dot_general(lagged, ref_block, (((0,), (0,)), ((), ())), preferred_el...  10.4 us
    all_to_all x1, waiting for transfers between devices, per_device(): lax.all_to_all(my_rows, 'ch', split_axis=1, concat_axis=0, tiled=True)  9.4 us
    all_to_all x1, starting transfers between devices, per_device(): lax.all_to_all(my_rows, 'ch', split_axis=1, concat_axis=0, tiled=True)  7.39 us
  transfers between devices with their start and end apart: 3, of which 3 were waited for; matrix products, arithmetic and copies ran while one was open for 1% of the time, Pallas kernels for 0%

commit v1 on v0

--- a/solution.py
+++ b/solution.py
@@ -1,9 +1,17 @@
+import functools
+import math
+
 import jax
 import jax.numpy as jnp
 from jax import lax
+from jax.experimental import pallas as pl
+from jax.experimental.pallas import tpu as pltpu
 from jax.sharding import PartitionSpec as P
 
 L = 64
+LANES = 128
+SHIFTS = 16
+MESH = pl.DeviceIdType.MESH
 
 
 def spread_2(block, axis, holder):
@@ -29,7 +37,7 @@
     return jnp.concatenate(pieces, axis=1)
 
 
-def per_device(strain, ref_local, owners):
+def narrow_blocks(strain, ref_local, owners):
     my_rows = strain[0]
     s_dev, chans = my_rows.shape
     n_ch = lax.axis_size("ch")
@@ -68,7 +76,290 @@
     return summed / (n_seg * (n_total - lag_ids))[:, None, None]
 
 
+def exchange_kernel(
+    n_seg, n_ch, group,
+    strain_hbm, owners_ref, local_ref, d_out, r_out,
+    mine, raw, rline, d_all, r_all,
+    load_sem, own_sem, a_send, a_recv, z_send, z_recv, p_send, p_recv, d_send, d_recv, r_send, r_recv,
+):
+    seg = lax.axis_index("seg")
+    me = lax.axis_index("ch")
+    high, low = me // group, me % group
+    n_high = n_ch // group
+    s_dev = strain_hbm.shape[0]
+    c_dev = strain_hbm.shape[1] // n_ch
+    half = s_dev // 2
+    n_total = s_dev * n_ch
+    n_panels, panel_w = local_ref.shape
+    width = n_panels * panel_w
+
+    barrier = pltpu.get_barrier_semaphore()
+    for k in range(1, n_ch):
+        pl.semaphore_signal(
+            barrier, inc=1, device_id=(seg, (me + k) % n_ch), device_id_type=MESH
+        )
+    for k in range(1, n_seg):
+        pl.semaphore_signal(
+            barrier, inc=1, device_id=((seg + k) % n_seg, me), device_id_type=MESH
+        )
+
+    load = pltpu.make_async_copy(strain_hbm, mine, load_sem)
+    load.start()
+    cols = pl.ds(pl.multiple_of(me * c_dev, LANES), c_dev)
+    own = pltpu.make_async_copy(strain_hbm.at[:, cols], raw.at[me], own_sem)
+    own.start()
+    load.wait()
+
+    blocks = []
+    for p in range(n_panels):
+        holder = jnp.full((s_dev, c_dev), owners_ref[p], jnp.int32)
+        block = jnp.zeros((s_dev, c_dev), jnp.float32)
+        for o in range(n_ch):
+            block = jnp.where(holder == o, mine[:, o * c_dev : (o + 1) * c_dev], block)
+        blocks.append(block)
+    blocks = jnp.concatenate(blocks, axis=1)
+    targets = jnp.concatenate(
+        [local_ref[p : p + 1, :] + p * c_dev for p in range(n_panels)], axis=1
+    )
+    hot = (
+        lax.broadcasted_iota(jnp.int32, (n_panels * c_dev, width), 0) == targets
+    ).astype(jnp.float32)
+    picked = jnp.dot(
+        blocks, hot, precision=lax.Precision.HIGHEST, preferred_element_type=jnp.float32
+    )
+    rline[low, high] = jnp.concatenate([picked[:half], picked[half:]], axis=1)
+
+    pl.semaphore_wait(barrier, n_ch - 1 + n_seg - 1)
+
+    z_copies = []
+    for k in range(1, n_high):
+        z_copies.append(
+            pltpu.make_async_remote_copy(
+                src_ref=rline.at[low, high],
+                dst_ref=rline.at[low, high],
+                send_sem=z_send.at[k],
+                recv_sem=z_recv.at[k],
+                device_id=(seg, ((high + k) % n_high) * group + low),
+                device_id_type=MESH,
+            )
+        )
+        z_copies[-1].start()
+    a_copies = []
+    for k in range(1, n_ch):
+        dst = (me + k) % n_ch
+        a_copies.append(
+            pltpu.make_async_remote_copy(
+                src_ref=strain_hbm.at[:, pl.ds(pl.multiple_of(dst * c_dev, LANES), c_dev)],
+                dst_ref=raw.at[me],
+                send_sem=a_send.at[k],
+                recv_sem=a_recv.at[k],
+                device_id=(seg, dst),
+                device_id_type=MESH,
+            )
+        )
+        a_copies[-1].start()
+
+    for copy in z_copies:
+        copy.wait()
+    p_copies = []
+    for k in range(1, group):
+        p_copies.append(
+            pltpu.make_async_remote_copy(
+                src_ref=rline.at[low],
+                dst_ref=rline.at[low],
+                send_sem=p_send.at[k],
+                recv_sem=p_recv.at[k],
+                device_id=(seg, high * group + (low + k) % group),
+                device_id_type=MESH,
+            )
+        )
+        p_copies[-1].start()
+    mid_time = (n_total - 1) / 2.0
+    spread = n_total * (n_total * n_total - 1) / 12.0
+
+    for copy in p_copies:
+        copy.wait()
+    rows = jnp.concatenate(
+        [rline[i % group, i // group] for i in range(n_ch)], axis=0
+    )
+    row_id = lax.broadcasted_iota(jnp.int32, (n_ch * half, LANES), 0)
+    upper = (lax.broadcasted_iota(jnp.int32, (n_ch * half, LANES), 1) >= width).astype(jnp.int32)
+    times = (row_id // half) * s_dev + row_id % half + upper * half
+    centred = times.astype(jnp.float32) - mid_time
+    level = jnp.sum(rows, axis=0, keepdims=True)
+    slope = jnp.sum(centred * rows, axis=0, keepdims=True)
+    level = (level + jnp.concatenate([level[:, width:], level[:, :width]], axis=1)) / n_total
+    slope = (slope + jnp.concatenate([slope[:, width:], slope[:, :width]], axis=1)) / spread
+    r_all[seg] = (rows - level - slope * centred).astype(jnp.bfloat16)
+    r_copies = []
+    for k in range(1, n_seg):
+        r_copies.append(
+            pltpu.make_async_remote_copy(
+                src_ref=r_all.at[seg],
+                dst_ref=r_all.at[seg],
+                send_sem=r_send.at[k],
+                recv_sem=r_recv.at[k],
+                device_id=((seg + k) % n_seg, me),
+                device_id_type=MESH,
+            )
+        )
+        r_copies[-1].start()
+
+    own.wait()
+    for copy in a_copies:
+        copy.wait()
+    series = raw[...].reshape(n_total, c_dev)
+    centred = lax.broadcasted_iota(jnp.int32, (n_total, c_dev), 0).astype(jnp.float32) - mid_time
+    level = jnp.sum(series, axis=0, keepdims=True) / n_total
+    slope = jnp.sum(centred * series, axis=0, keepdims=True) / spread
+    d_all[seg] = (series - level - slope * centred).astype(jnp.bfloat16)
+    d_copies = []
+    for k in range(1, n_seg):
+        d_copies.append(
+            pltpu.make_async_remote_copy(
+                src_ref=d_all.at[seg],
+                dst_ref=d_all.at[seg],
+                send_sem=d_send.at[k],
+                recv_sem=d_recv.at[k],
+                device_id=((seg + k) % n_seg, me),
+                device_id_type=MESH,
+            )
+        )
+        d_copies[-1].start()
+    for copy in r_copies:
+        copy.wait()
+    r_out[...] = r_all[...]
+    for copy in d_copies:
+        copy.wait()
+    d_out[...] = d_all[...]
+
+
+def lag_kernel(n_seg, half, d_ref, r_ref, out_ref, d_pad, shifted):
+    lag_dev, width, c_dev = out_ref.shape
+    n_total = d_ref.shape[1]
+    n_ch = n_total // (2 * half)
+    seg = lax.axis_index("seg")
+    steps = lag_dev // SHIFTS
+    d_pad[:, n_total:, :] = jnp.zeros((n_seg, L, c_dev), d_pad.dtype)
+    d_pad[:, :n_total, :] = d_ref[...]
+    shifted[:, : SHIFTS + 8, :] = jnp.zeros((n_seg, SHIFTS + 8, LANES), jnp.float32)
+    lefts, rights = [], []
+    for s in range(n_seg):
+        packed = r_ref[s].astype(jnp.float32)
+        swapped = pltpu.roll(packed, width, 1)
+        both = jnp.concatenate(
+            [packed.reshape(n_ch, half, LANES), swapped.reshape(n_ch, half, LANES)], axis=1
+        ).reshape(n_total, LANES)
+        turned = jnp.concatenate(
+            [swapped.reshape(n_ch, half, LANES), packed.reshape(n_ch, half, LANES)], axis=1
+        ).reshape(n_total, LANES)
+        shifted[s, pl.ds(SHIFTS, n_total), 0:width] = both[:, :width]
+        shifted[s, pl.ds(SHIFTS + 1, n_total), width:LANES] = turned[:, width:]
+        lefts.append(
+            jnp.concatenate(
+                [
+                    d_pad[
+                        s,
+                        pl.ds(pl.multiple_of(seg * lag_dev + a * SHIFTS, SHIFTS), n_total),
+                        :,
+                    ]
+                    for a in range(steps)
+                ],
+                axis=1,
+            )
+        )
+    base = (seg * lag_dev).astype(jnp.float32)
+    quad = 4
+    for j in range(SHIFTS // quad):
+        total = None
+        for s in range(n_seg):
+            right = jnp.concatenate(
+                [
+                    shifted[s, pl.ds(SHIFTS - quad * j - b, n_total), :].astype(jnp.bfloat16)
+                    for b in range(0, quad, 2)
+                ],
+                axis=1,
+            )
+            part = lax.dot_general(
+                lefts[s], right, (((0,), (0,)), ((), ())), preferred_element_type=jnp.float32
+            )
+            total = part if total is None else total + part
+        turned = total.T
+        for a in range(steps):
+            for b in range(quad):
+                k = a * SHIFTS + j * quad + b
+                block = turned[b * width : (b + 1) * width, a * c_dev : (a + 1) * c_dev]
+                out_ref[k] = block / (n_seg * (n_total - (base + k)))
+
+
+def wide_blocks(strain, ref_local, owners):
+    my_rows = strain[0]
+    s_dev, chans = my_rows.shape
+    n_ch = lax.axis_size("ch")
+    n_seg = lax.axis_size("seg")
+    n_total = s_dev * n_ch
+    c_dev = chans // n_ch
+    half = s_dev // 2
+    group = max(g for g in range(1, math.isqrt(n_ch) + 1) if n_ch % g == 0)
+    n_high = n_ch // group
+    width = ref_local.shape[0] * ref_local.shape[1]
+    vmem = pl.BlockSpec(memory_space=pltpu.VMEM)
+    dma = pltpu.SemaphoreType.DMA
+    d_shape = (n_seg, n_total, c_dev)
+    r_shape = (n_seg, n_ch * half, LANES)
+    d_all, r_all = pl.pallas_call(
+        functools.partial(exchange_kernel, n_seg, n_ch, group),
+        out_shape=(
+            jax.ShapeDtypeStruct(d_shape, jnp.bfloat16),
+            jax.ShapeDtypeStruct(r_shape, jnp.bfloat16),
+        ),
+        in_specs=[
+            pl.BlockSpec(memory_space=pl.ANY),
+            pl.BlockSpec(memory_space=pltpu.SMEM),
+            vmem,
+        ],
+        out_specs=(vmem, vmem),
+        scratch_shapes=[
+            pltpu.VMEM((s_dev, chans), jnp.float32),
+            pltpu.VMEM((n_ch, s_dev, c_dev), jnp.float32),
+            pltpu.VMEM((group, n_high, half, LANES), jnp.float32),
+            pltpu.VMEM(d_shape, jnp.bfloat16),
+            pltpu.VMEM(r_shape, jnp.bfloat16),
+            dma, dma,
+            dma((n_ch,)), dma((n_ch,)),
+            dma((n_high,)), dma((n_high,)),
+            dma((group,)), dma((group,)),
+            dma((n_seg,)), dma((n_seg,)),
+            dma((n_seg,)), dma((n_seg,)),
+        ],
+        compiler_params=pltpu.CompilerParams(collective_id=0, has_side_effects=True),
+    )(my_rows, owners, ref_local)
+    turned = pl.pallas_call(
+        functools.partial(lag_kernel, n_seg, half),
+        out_shape=jax.ShapeDtypeStruct((L // n_seg, width, c_dev), jnp.float32),
+        in_specs=[vmem, vmem],
+        out_specs=vmem,
+        scratch_shapes=[
+            pltpu.VMEM((n_seg, n_total + L, c_dev), jnp.bfloat16),
+            pltpu.VMEM((n_seg, SHIFTS + n_total + 8, LANES), jnp.float32),
+        ],
+    )(d_all, r_all)
+    return turned.transpose(0, 2, 1)
+
+
 def solution(mesh):
+    n_seg, n_ch = mesh.shape["seg"], mesh.shape["ch"]
+
+    def per_device(strain, ref_local, owners):
+        s_dev, chans = strain.shape[1:]
+        fits = (
+            (chans // n_ch) % LANES == 0
+            and (L // n_seg) % SHIFTS == 0
+            and s_dev % 32 == 0
+            and 2 * ref_local.size == LANES
+        )
+        return (wide_blocks if fits else narrow_blocks)(strain, ref_local, owners)
+
     in_specs = (P("seg", "ch", None), P(), P())
     out_specs = P("seg", "ch", None)
     return jax.shard_map(

time: 273 us -> 34.3 us (0.13)
  the two profiles are of different devices: /device:TPU:0 before, /device:TPU:3 now
where the time goes in v1:
time: 34.3 us; the launch traced here: 34.1 us
  Pallas kernels  34.1 us (99%)
    pallas_call x1, Pallas kernels, wide_blocks(): pl.pallas_call(functools.partial(exchange_kernel, n_seg, n_ch, group), ou...  30.4 us
    pallas_call x1, Pallas kernels, wide_blocks(): pl.pallas_call(functools.partial(lag_kernel, n_seg, half), out_shape=jax....  3.66 us

profile of v1, /device:TPU:3, one launch (start us, length us, event | category | flops | bytes accessed | tf_op | source)
XLA Modules:
  0.0 34.1 jit_solution(6582050659103294839)
XLA Ops:
  0.0 30.4 %shard_map.37 = (bf16[2,1024,128]{2,1,0:T(8,128)(2,1)}, bf16[2,512,128]{2,1,0:T(8,128)(2,1)}) custom-call(f32[64,2048]{1,0:T(8,128)} %bitcast.2, s32[4]{0:T(128)} %owners_ref.1, s32[4,16]{1,0:T(4,128)} %local_ref.1), custom_call_target="tpu_custom_call" | custom-call | tf_op jit(solution)/shard_map/pallas_call | solution.py:310
  30.4 3.7 %shard_map.38 = f32[32,64,128]{2,1,0:T(8,128)} custom-call(bf16[2,1024,128]{2,1,0:T(8,128)(2,1)} %get-tuple-element.7.d_ref, bf16[2,512,128]{2,1,0:T(8,128)(2,1)} %get-tuple-element.8.r_ref), custom_call_target="tpu_custom_call" | custom-call | tf_op jit(solution)/shard_map/pallas_call | solution.py:337

commit v2 on v1

--- a/solution.py
+++ b/solution.py
@@ -11,6 +11,7 @@
 L = 64
 LANES = 128
 SHIFTS = 16
+GRANT = 24 * 1024 * 1024
 MESH = pl.DeviceIdType.MESH
 
 
@@ -79,8 +80,9 @@
 def exchange_kernel(
     n_seg, n_ch, group,
     strain_hbm, owners_ref, local_ref, d_out, r_out,
-    mine, raw, rline, d_all, r_all,
-    load_sem, own_sem, a_send, a_recv, z_send, z_recv, p_send, p_recv, d_send, d_recv, r_send, r_recv,
+    mine, raw, rline, d_all, r_all, stat_out, stat_in,
+    load_sem, own_sem, s_send, s_recv, a_send, a_recv, z_send, z_recv, p_send, p_recv,
+    d_send, d_recv, r_send, r_recv,
 ):
     seg = lax.axis_index("seg")
     me = lax.axis_index("ch")
@@ -92,9 +94,24 @@
     n_total = s_dev * n_ch
     n_panels, panel_w = local_ref.shape
     width = n_panels * panel_w
+    mid_time = (n_total - 1) / 2.0
+    spread = n_total * (n_total * n_total - 1) / 12.0
+    order = sorted(range(1, n_ch), key=lambda k: -min(k, n_ch - k))
+
+    def remote(src, dst, sems, k, seg_to, ch_to):
+        copy = pltpu.make_async_remote_copy(
+            src_ref=src,
+            dst_ref=dst,
+            send_sem=sems[0].at[k],
+            recv_sem=sems[1].at[k],
+            device_id=(seg_to, ch_to),
+            device_id_type=MESH,
+        )
+        copy.start()
+        return copy
 
     barrier = pltpu.get_barrier_semaphore()
-    for k in range(1, n_ch):
+    for k in order:
         pl.semaphore_signal(
             barrier, inc=1, device_id=(seg, (me + k) % n_ch), device_id_type=MESH
         )
@@ -109,6 +126,19 @@
     own = pltpu.make_async_copy(strain_hbm.at[:, cols], raw.at[me], own_sem)
     own.start()
     load.wait()
+
+    my_times = (
+        lax.broadcasted_iota(jnp.int32, (s_dev, c_dev), 0) + me * s_dev
+    ).astype(jnp.float32) - mid_time
+    for o in range(n_ch):
+        block = mine[:, o * c_dev : (o + 1) * c_dev]
+        stat_out[o] = jnp.concatenate(
+            [
+                jnp.sum(block, axis=0, keepdims=True),
+                jnp.sum(my_times * block, axis=0, keepdims=True),
+            ],
+            axis=0,
+        )
 
     blocks = []
     for p in range(n_panels):
@@ -128,110 +158,95 @@
         blocks, hot, precision=lax.Precision.HIGHEST, preferred_element_type=jnp.float32
     )
     rline[low, high] = jnp.concatenate([picked[:half], picked[half:]], axis=1)
+    stat_in[me] = stat_out[me]
 
     pl.semaphore_wait(barrier, n_ch - 1 + n_seg - 1)
 
+    s_copies = []
+    for k in order:
+        dst = (me + k) % n_ch
+        s_copies.append(
+            remote(stat_out.at[dst], stat_in.at[me], (s_send, s_recv), k, seg, dst)
+        )
     z_copies = []
     for k in range(1, n_high):
-        z_copies.append(
-            pltpu.make_async_remote_copy(
-                src_ref=rline.at[low, high],
-                dst_ref=rline.at[low, high],
-                send_sem=z_send.at[k],
-                recv_sem=z_recv.at[k],
-                device_id=(seg, ((high + k) % n_high) * group + low),
-                device_id_type=MESH,
-            )
-        )
-        z_copies[-1].start()
+        block = rline.at[low, high]
+        dst = ((high + k) % n_high) * group + low
+        z_copies.append(remote(block, block, (z_send, z_recv), k, seg, dst))
     a_copies = []
-    for k in range(1, n_ch):
+    for k in order:
         dst = (me + k) % n_ch
-        a_copies.append(
-            pltpu.make_async_remote_copy(
-                src_ref=strain_hbm.at[:, pl.ds(pl.multiple_of(dst * c_dev, LANES), c_dev)],
-                dst_ref=raw.at[me],
-                send_sem=a_send.at[k],
-                recv_sem=a_recv.at[k],
-                device_id=(seg, dst),
-                device_id_type=MESH,
-            )
-        )
-        a_copies[-1].start()
+        block = strain_hbm.at[:, pl.ds(pl.multiple_of(dst * c_dev, LANES), c_dev)]
+        a_copies.append(remote(block, raw.at[me], (a_send, a_recv), k, seg, dst))
 
     for copy in z_copies:
         copy.wait()
     p_copies = []
     for k in range(1, group):
-        p_copies.append(
-            pltpu.make_async_remote_copy(
-                src_ref=rline.at[low],
-                dst_ref=rline.at[low],
-                send_sem=p_send.at[k],
-                recv_sem=p_recv.at[k],
-                device_id=(seg, high * group + (low + k) % group),
-                device_id_type=MESH,
-            )
-        )
-        p_copies[-1].start()
-    mid_time = (n_total - 1) / 2.0
-    spread = n_total * (n_total * n_total - 1) / 12.0
-
-    for copy in p_copies:
+        block = rline.at[low]
+        dst = high * group + (low + k) % group
+        p_copies.append(remote(block, block, (p_send, p_recv), k, seg, dst))
+
+    for copy in s_copies:
         copy.wait()
-    rows = jnp.concatenate(
-        [rline[i % group, i // group] for i in range(n_ch)], axis=0
-    )
-    row_id = lax.broadcasted_iota(jnp.int32, (n_ch * half, LANES), 0)
-    upper = (lax.broadcasted_iota(jnp.int32, (n_ch * half, LANES), 1) >= width).astype(jnp.int32)
-    times = (row_id // half) * s_dev + row_id % half + upper * half
-    centred = times.astype(jnp.float32) - mid_time
-    level = jnp.sum(rows, axis=0, keepdims=True)
-    slope = jnp.sum(centred * rows, axis=0, keepdims=True)
-    level = (level + jnp.concatenate([level[:, width:], level[:, :width]], axis=1)) / n_total
-    slope = (slope + jnp.concatenate([slope[:, width:], slope[:, :width]], axis=1)) / spread
-    r_all[seg] = (rows - level - slope * centred).astype(jnp.bfloat16)
+    sums = jnp.sum(stat_in[...], axis=0)
+    level_d = sums[0:1] / n_total
+    slope_d = sums[1:2] / spread
+
     r_copies = []
-    for k in range(1, n_seg):
-        r_copies.append(
-            pltpu.make_async_remote_copy(
-                src_ref=r_all.at[seg],
-                dst_ref=r_all.at[seg],
-                send_sem=r_send.at[k],
-                recv_sem=r_recv.at[k],
-                device_id=((seg + k) % n_seg, me),
-                device_id_type=MESH,
-            )
-        )
-        r_copies[-1].start()
-
-    own.wait()
-    for copy in a_copies:
-        copy.wait()
-    series = raw[...].reshape(n_total, c_dev)
-    centred = lax.broadcasted_iota(jnp.int32, (n_total, c_dev), 0).astype(jnp.float32) - mid_time
-    level = jnp.sum(series, axis=0, keepdims=True) / n_total
-    slope = jnp.sum(centred * series, axis=0, keepdims=True) / spread
-    d_all[seg] = (series - level - slope * centred).astype(jnp.bfloat16)
     d_copies = []
-    for k in range(1, n_seg):
-        d_copies.append(
-            pltpu.make_async_remote_copy(
-                src_ref=d_all.at[seg],
-                dst_ref=d_all.at[seg],
-                send_sem=d_send.at[k],
-                recv_sem=d_recv.at[k],
-                device_id=((seg + k) % n_seg, me),
-                device_id_type=MESH,
-            )
-        )
-        d_copies[-1].start()
+
+    def forward(k):
+        block = d_all.at[seg, (me - k + n_ch) % n_ch]
+        for j in range(1, n_seg):
+            d_copies.append(
+                remote(block, block, (d_send.at[j], d_recv.at[j]), k, (seg + j) % n_seg, me)
+            )
+
+    ready = None
+    for place, k in enumerate([0] + order):
+        if k == 0:
+            own.wait()
+        else:
+            a_copies[place - 1].wait()
+        source = (me - k + n_ch) % n_ch
+        times = (
+            lax.broadcasted_iota(jnp.int32, (s_dev, c_dev), 0) + source * s_dev
+        ).astype(jnp.float32) - mid_time
+        d_all[seg, source] = (raw[source] - level_d - slope_d * times).astype(jnp.bfloat16)
+        if ready is not None:
+            forward(ready)
+        ready = k
+        if place == n_ch // 2:
+            for copy in p_copies:
+                copy.wait()
+            rows = jnp.concatenate(
+                [rline[i % group, i // group] for i in range(n_ch)], axis=0
+            )
+            row_id = lax.broadcasted_iota(jnp.int32, (n_ch * half, LANES), 0)
+            upper = (
+                lax.broadcasted_iota(jnp.int32, (n_ch * half, LANES), 1) >= width
+            ).astype(jnp.int32)
+            times = (row_id // half) * s_dev + row_id % half + upper * half
+            centred = times.astype(jnp.float32) - mid_time
+            level = jnp.sum(rows, axis=0, keepdims=True)
+            slope = jnp.sum(centred * rows, axis=0, keepdims=True)
+            level = (level + pltpu.roll(level, width, 1)) / n_total
+            slope = (slope + pltpu.roll(slope, width, 1)) / spread
+            r_all[seg] = (rows - level - slope * centred).astype(jnp.bfloat16)
+        if place == n_ch // 2 + 1:
+            block = r_all.at[seg]
+            for j in range(1, n_seg):
+                r_copies.append(
+                    remote(block, block, (r_send, r_recv), j, (seg + j) % n_seg, me)
+                )
+    forward(ready)
     for copy in r_copies:
         copy.wait()
     r_out[...] = r_all[...]
     for copy in d_copies:
         copy.wait()
-    d_out[...] = d_all[...]
+    d_out[...] = d_all[...].reshape(d_out.shape)
 
 
 def lag_kernel(n_seg, half, d_ref, r_ref, out_ref, d_pad, shifted):
@@ -323,16 +338,19 @@
             pltpu.VMEM((s_dev, chans), jnp.float32),
             pltpu.VMEM((n_ch, s_dev, c_dev), jnp.float32),
             pltpu.VMEM((group, n_high, half, LANES), jnp.float32),
-            pltpu.VMEM(d_shape, jnp.bfloat16),
+            pltpu.VMEM((n_seg, n_ch, s_dev, c_dev), jnp.bfloat16),
             pltpu.VMEM(r_shape, jnp.bfloat16),
+            pltpu.VMEM((n_ch, 2, c_dev), jnp.float32),
+            pltpu.VMEM((n_ch, 2, c_dev), jnp.float32),
             dma, dma,
+            dma((n_ch,)), dma((n_ch,)),
             dma((n_ch,)), dma((n_ch,)),
             dma((n_high,)), dma((n_high,)),
             dma((group,)), dma((group,)),
-            dma((n_seg,)), dma((n_seg,)),
+            dma((n_seg, n_ch)), dma((n_seg, n_ch)),
             dma((n_seg,)), dma((n_seg,)),
         ],
-        compiler_params=pltpu.CompilerParams(collective_id=0, has_side_effects=True),
+        compiler_params=pltpu.CompilerParams(collective_id=0, has_side_effects=True, vmem_limit_bytes=GRANT),
     )(my_rows, owners, ref_local)
     turned = pl.pallas_call(
         functools.partial(lag_kernel, n_seg, half),
@@ -343,6 +361,7 @@
             pltpu.VMEM((n_seg, n_total + L, c_dev), jnp.bfloat16),
             pltpu.VMEM((n_seg, SHIFTS + n_total + 8, LANES), jnp.float32),
         ],
+        compiler_params=pltpu.CompilerParams(vmem_limit_bytes=GRANT),
     )(d_all, r_all)
     return turned.transpose(0, 2, 1)
 

time: 34.3 us -> 34.6 us (level)
  the two profiles are of different devices: /device:TPU:3 before, /device:TPU:0 now
where the time goes in v2:
time: 34.6 us; the launch traced here: 34.4 us
  Pallas kernels  32 us (92%)
  local copies, waits for them, and re-layouts  2.38 us (7%)
    pallas_call x1, Pallas kernels, wide_blocks(): pl.pallas_call(functools.partial(exchange_kernel, n_seg, n_ch, group), ou...  29.5 us
    pallas_call x1, Pallas kernels, wide_blocks(): pl.pallas_call(functools.partial(lag_kernel, n_seg, half), out_shape=jax....  2.56 us
    unnamed x6, local copies, waits for them, and re-layouts  2.38 us

profile of v2, /device:TPU:0, one launch (start us, length us, event | category | flops | bytes accessed | tf_op | source)
XLA Modules:
  0.0 34.4 jit_solution(17567349080894201313)
XLA Ops:
  0.0 0.0 copy-start.2
  0.0 0.7 %copy-done.2 = s32[4]{0:T(128)S(1)} copy-done((s32[4]{0:T(128)S(1)}, s32[4]{0:T(128)}, u32[]{:S(2)}) %copy-start.2) | copy-done | bytes 40
  0.7 0.0 copy-start
  0.7 1.0 %copy-done = f32[1,64,2048]{2,1,0:T(8,128)S(1)} copy-done((f32[1,64,2048]{2,1,0:T(8,128)S(1)}, f32[1,64,2048]{2,1,0:T(8,128)}, u32[]{:S(2)}) %copy-start) | copy-done | bytes 524312
  1.7 0.0 copy-start.1
  1.7 0.7 %copy-done.1 = s32[4,16]{1,0:T(4,128)S(1)} copy-done((s32[4,16]{1,0:T(4,128)S(1)}, s32[4,16]{1,0:T(4,128)}, u32[]{:S(2)}) %copy-start.1) | copy-done | bytes 280
  2.4 29.5 %shard_map.37 = (bf16[2,1024,128]{2,1,0:T(8,128)(2,1)S(1)}, bf16[2,512,128]{2,1,0:T(8,128)(2,1)S(1)}) custom-call(f32[64,2048]{1,0:T(8,128)S(1)} %bitcast.2, s32[4]{0:T(128)S(1)} %copy-done.2, s32[4,16]{1,0:T(4,128)S(1)} %copy-done.1), custom_call_target="tpu_custom_call" | custom-call | tf_op jit(solution)/shard_map/pallas_call | solution.py:325
  31.9 2.6 %shard_map.38 = f32[32,64,128]{2,1,0:T(8,128)} custom-call(bf16[2,1024,128]{2,1,0:T(8,128)(2,1)S(1)} %get-tuple-element.7.d_ref, bf16[2,512,128]{2,1,0:T(8,128)(2,1)S(1)} %get-tuple-element.8.r_ref), custom_call_target="tpu_custom_call" | custom-call | tf_op jit(solution)/shard_map/pallas_call | solution.py:355
Async XLA Ops:
  0.0 0.7 %copy-start.2 = (s32[4]{0:T(128)S(1)}, s32[4]{0:T(128)}, u32[]{:S(2)}) copy-start(s32[4]{0:T(128)} %owners_ref.1) | copy-start | bytes 52
  0.7 1.0 %copy-start = (f32[1,64,2048]{2,1,0:T(8,128)S(1)}, f32[1,64,2048]{2,1,0:T(8,128)}, u32[]{:S(2)}) copy-start(f32[1,64,2048]{2,1,0:T(8,128)} %param.3) | copy-start | bytes 1572868
  1.7 0.7 %copy-start.1 = (s32[4,16]{1,0:T(4,128)S(1)}, s32[4,16]{1,0:T(4,128)}, u32[]{:S(2)}) copy-start(s32[4,16]{1,0:T(4,128)} %local_ref.1) | copy-start | bytes 772

commit v3 on v2

--- a/solution.py
+++ b/solution.py
@@ -79,9 +79,9 @@
 
 def exchange_kernel(
     n_seg, n_ch, group,
-    strain_hbm, owners_ref, local_ref, d_out, r_out,
-    mine, raw, rline, d_all, r_all, stat_out, stat_in,
-    load_sem, own_sem, s_send, s_recv, a_send, a_recv, z_send, z_recv, p_send, p_recv,
+    strain_hbm, owners_hbm, local_hbm, d_out, r_out,
+    owners_ref, local_ref, mine, raw, rline, d_all, r_all, stat_out, stat_in,
+    load_sem, own_sem, owners_sem, local_sem, s_send, s_recv, a_send, a_recv, z_send, z_recv, p_send, p_recv,
     d_send, d_recv, r_send, r_recv,
 ):
     seg = lax.axis_index("seg")
@@ -96,7 +96,15 @@
     width = n_panels * panel_w
     mid_time = (n_total - 1) / 2.0
     spread = n_total * (n_total * n_total - 1) / 12.0
-    order = sorted(range(1, n_ch), key=lambda k: -min(k, n_ch - k))
+    order = list(range(1, n_ch))
+
+    def partner(k):
+        place, bit = me, 1
+        while bit <= k:
+            if k & bit:
+                place = place + (1 - 2 * ((me // bit) % 2)) * bit
+            bit *= 2
+        return place
 
     def remote(src, dst, sems, k, seg_to, ch_to):
         copy = pltpu.make_async_remote_copy(
@@ -113,7 +121,7 @@
     barrier = pltpu.get_barrier_semaphore()
     for k in order:
         pl.semaphore_signal(
-            barrier, inc=1, device_id=(seg, (me + k) % n_ch), device_id_type=MESH
+            barrier, inc=1, device_id=(seg, partner(k)), device_id_type=MESH
         )
     for k in range(1, n_seg):
         pl.semaphore_signal(
@@ -122,6 +130,10 @@
 
     load = pltpu.make_async_copy(strain_hbm, mine, load_sem)
     load.start()
+    load_owners = pltpu.make_async_copy(owners_hbm, owners_ref, owners_sem)
+    load_owners.start()
+    load_local = pltpu.make_async_copy(local_hbm, local_ref, local_sem)
+    load_local.start()
     cols = pl.ds(pl.multiple_of(me * c_dev, LANES), c_dev)
     own = pltpu.make_async_copy(strain_hbm.at[:, cols], raw.at[me], own_sem)
     own.start()
@@ -140,6 +152,8 @@
             axis=0,
         )
 
+    load_owners.wait()
+    load_local.wait()
     blocks = []
     for p in range(n_panels):
         holder = jnp.full((s_dev, c_dev), owners_ref[p], jnp.int32)
@@ -164,7 +178,7 @@
 
     s_copies = []
     for k in order:
-        dst = (me + k) % n_ch
+        dst = partner(k)
         s_copies.append(
             remote(stat_out.at[dst], stat_in.at[me], (s_send, s_recv), k, seg, dst)
         )
@@ -175,7 +189,7 @@
         z_copies.append(remote(block, block, (z_send, z_recv), k, seg, dst))
     a_copies = []
     for k in order:
-        dst = (me + k) % n_ch
+        dst = partner(k)
         block = strain_hbm.at[:, pl.ds(pl.multiple_of(dst * c_dev, LANES), c_dev)]
         a_copies.append(remote(block, raw.at[me], (a_send, a_recv), k, seg, dst))
 
@@ -197,7 +211,7 @@
     d_copies = []
 
     def forward(k):
-        block = d_all.at[seg, (me - k + n_ch) % n_ch]
+        block = d_all.at[seg, partner(k)]
         for j in range(1, n_seg):
             d_copies.append(
                 remote(block, block, (d_send.at[j], d_recv.at[j]), k, (seg + j) % n_seg, me)
@@ -209,7 +223,7 @@
             own.wait()
         else:
             a_copies[place - 1].wait()
-        source = (me - k + n_ch) % n_ch
+        source = partner(k)
         times = (
             lax.broadcasted_iota(jnp.int32, (s_dev, c_dev), 0) + source * s_dev
         ).astype(jnp.float32) - mid_time
@@ -328,13 +342,11 @@
             jax.ShapeDtypeStruct(d_shape, jnp.bfloat16),
             jax.ShapeDtypeStruct(r_shape, jnp.bfloat16),
         ),
-        in_specs=[
-            pl.BlockSpec(memory_space=pl.ANY),
-            pl.BlockSpec(memory_space=pltpu.SMEM),
-            vmem,
-        ],
+        in_specs=[pl.BlockSpec(memory_space=pltpu.HBM)] * 3,
         out_specs=(vmem, vmem),
         scratch_shapes=[
+            pltpu.SMEM(owners.shape, jnp.int32),
+            pltpu.VMEM(ref_local.shape, jnp.int32),
             pltpu.VMEM((s_dev, chans), jnp.float32),
             pltpu.VMEM((n_ch, s_dev, c_dev), jnp.float32),
             pltpu.VMEM((group, n_high, half, LANES), jnp.float32),
@@ -342,7 +354,7 @@
             pltpu.VMEM(r_shape, jnp.bfloat16),
             pltpu.VMEM((n_ch, 2, c_dev), jnp.float32),
             pltpu.VMEM((n_ch, 2, c_dev), jnp.float32),
-            dma, dma,
+            dma, dma, dma, dma,
             dma((n_ch,)), dma((n_ch,)),
             dma((n_ch,)), dma((n_ch,)),
             dma((n_high,)), dma((n_high,)),
@@ -375,6 +387,7 @@
             (chans // n_ch) % LANES == 0
             and (L // n_seg) % SHIFTS == 0
             and s_dev % 32 == 0
+            and n_ch & (n_ch - 1) == 0
             and 2 * ref_local.size == LANES
         )
         return (wide_blocks if fits else narrow_blocks)(strain, ref_local, owners)

time: 34.6 us -> 29.6 us (0.86)
  Pallas kernels: 32 us -> 27 us
    pallas_call x1, Pallas kernels: 29.5 us -> 24.5 us  [wide_blocks(): pl.pallas_call(functools.partial(exchange_kernel, n_seg, n_ch, group), ou...]
where the time goes in v3:
time: 29.6 us; the launch traced here: 29.4 us
  Pallas kernels  27 us (91%)
  local copies, waits for them, and re-layouts  2.38 us (8%)
    pallas_call x1, Pallas kernels, wide_blocks(): pl.pallas_call(functools.partial(exchange_kernel, n_seg, n_ch, group), ou...  24.5 us
    pallas_call x1, Pallas kernels, wide_blocks(): pl.pallas_call(functools.partial(lag_kernel, n_seg, half), out_shape=jax....  2.57 us
    unnamed x6, local copies, waits for them, and re-layouts  2.38 us

profile of v3, /device:TPU:0, one launch (start us, length us, event | category | flops | bytes accessed | tf_op | source)
XLA Modules:
  0.0 29.4 jit_solution(4639644316199726596)
XLA Ops:
  0.0 0.0 copy-start.2
  0.0 0.7 %copy-done.2 = s32[4]{0:T(128)S(1)} copy-done((s32[4]{0:T(128)S(1)}, s32[4]{0:T(128)}, u32[]{:S(2)}) %copy-start.2) | copy-done | bytes 40
  0.7 0.0 copy-start
  0.7 1.0 %copy-done = f32[1,64,2048]{2,1,0:T(8,128)S(1)} copy-done((f32[1,64,2048]{2,1,0:T(8,128)S(1)}, f32[1,64,2048]{2,1,0:T(8,128)}, u32[]{:S(2)}) %copy-start) | copy-done | bytes 524312
  1.7 0.0 copy-start.1
  1.7 0.7 %copy-done.1 = s32[4,16]{1,0:T(4,128)S(1)} copy-done((s32[4,16]{1,0:T(4,128)S(1)}, s32[4,16]{1,0:T(4,128)}, u32[]{:S(2)}) %copy-start.1) | copy-done | bytes 280
  2.4 24.5 %shard_map.37 = (bf16[2,1024,128]{2,1,0:T(8,128)(2,1)S(1)}, bf16[2,512,128]{2,1,0:T(8,128)(2,1)S(1)}) custom-call(f32[64,2048]{1,0:T(8,128)S(1)} %bitcast.2, s32[4]{0:T(128)S(1)} %copy-done.2, s32[4,16]{1,0:T(4,128)S(1)} %copy-done.1), custom_call_target="tpu_custom_call" | custom-call | tf_op jit(solution)/shard_map/pallas_call | solution.py:339
  26.8 2.6 %shard_map.38 = f32[32,64,128]{2,1,0:T(8,128)} custom-call(bf16[2,1024,128]{2,1,0:T(8,128)(2,1)S(1)} %get-tuple-element.7.d_ref, bf16[2,512,128]{2,1,0:T(8,128)(2,1)S(1)} %get-tuple-element.8.r_ref), custom_call_target="tpu_custom_call" | custom-call | tf_op jit(solution)/shard_map/pallas_call | solution.py:367
Async XLA Ops:
  0.0 0.7 %copy-start.2 = (s32[4]{0:T(128)S(1)}, s32[4]{0:T(128)}, u32[]{:S(2)}) copy-start(s32[4]{0:T(128)} %owners_hbm.1) | copy-start | bytes 52
  0.7 1.0 %copy-start = (f32[1,64,2048]{2,1,0:T(8,128)S(1)}, f32[1,64,2048]{2,1,0:T(8,128)}, u32[]{:S(2)}) copy-start(f32[1,64,2048]{2,1,0:T(8,128)} %param.3) | copy-start | bytes 1572868
  1.7 0.7 %copy-start.1 = (s32[4,16]{1,0:T(4,128)S(1)}, s32[4,16]{1,0:T(4,128)}, u32[]{:S(2)}) copy-start(s32[4,16]{1,0:T(4,128)} %local_hbm.1) | copy-start | bytes 772

commit v4 on v3

--- a/solution.py
+++ b/solution.py
@@ -82,7 +82,7 @@
     strain_hbm, owners_hbm, local_hbm, d_out, r_out,
     owners_ref, local_ref, mine, raw, rline, d_all, r_all, stat_out, stat_in,
     load_sem, own_sem, owners_sem, local_sem, s_send, s_recv, a_send, a_recv, z_send, z_recv, p_send, p_recv,
-    d_send, d_recv, r_send, r_recv,
+    d_send, d_recv, r_send, r_recv, c_send, c_recv,
 ):
     seg = lax.axis_index("seg")
     me = lax.axis_index("ch")
@@ -247,17 +247,24 @@
             slope = jnp.sum(centred * rows, axis=0, keepdims=True)
             level = (level + pltpu.roll(level, width, 1)) / n_total
             slope = (slope + pltpu.roll(slope, width, 1)) / spread
-            r_all[seg] = (rows - level - slope * centred).astype(jnp.bfloat16)
+            r_all[seg] = (
+                (rows - level - slope * centred).astype(jnp.bfloat16).reshape(r_all.shape[1:])
+            )
         if place == n_ch // 2 + 1:
-            block = r_all.at[seg]
+            block = r_all.at[seg, me % 2]
             for j in range(1, n_seg):
                 r_copies.append(
                     remote(block, block, (r_send, r_recv), j, (seg + j) % n_seg, me)
                 )
     forward(ready)
-    for copy in r_copies:
+    c_copies = []
+    for j, copy in enumerate(r_copies, 1):
         copy.wait()
-    r_out[...] = r_all[...]
+        block = r_all.at[(seg - j + n_seg) % n_seg, me % 2]
+        c_copies.append(remote(block, block, (c_send, c_recv), j, seg, partner(1)))
+    for copy in c_copies:
+        copy.wait()
+    r_out[...] = r_all[...].reshape(r_out.shape)
     for copy in d_copies:
         copy.wait()
     d_out[...] = d_all[...].reshape(d_out.shape)
@@ -351,7 +358,7 @@
             pltpu.VMEM((n_ch, s_dev, c_dev), jnp.float32),
             pltpu.VMEM((group, n_high, half, LANES), jnp.float32),
             pltpu.VMEM((n_seg, n_ch, s_dev, c_dev), jnp.bfloat16),
-            pltpu.VMEM(r_shape, jnp.bfloat16),
+            pltpu.VMEM((n_seg, 2, n_ch * half // 2, LANES), jnp.bfloat16),
             pltpu.VMEM((n_ch, 2, c_dev), jnp.float32),
             pltpu.VMEM((n_ch, 2, c_dev), jnp.float32),
             dma, dma, dma, dma,
@@ -360,6 +367,7 @@
             dma((n_high,)), dma((n_high,)),
             dma((group,)), dma((group,)),
             dma((n_seg, n_ch)), dma((n_seg, n_ch)),
+            dma((n_seg,)), dma((n_seg,)),
             dma((n_seg,)), dma((n_seg,)),
         ],
         compiler_params=pltpu.CompilerParams(collective_id=0, has_side_effects=True, vmem_limit_bytes=GRANT),
@@ -387,6 +395,7 @@
             (chans // n_ch) % LANES == 0
             and (L // n_seg) % SHIFTS == 0
             and s_dev % 32 == 0
+            and n_ch % 2 == 0
             and n_ch & (n_ch - 1) == 0
             and 2 * ref_local.size == LANES
         )

time: 29.6 us -> 28 us (0.946)
  Pallas kernels: 27 us -> 25.4 us
    pallas_call x1, Pallas kernels: 24.5 us -> 22.8 us  [wide_blocks(): pl.pallas_call(functools.partial(exchange_kernel, n_seg, n_ch, group), ou...]
where the time goes in v4:
time: 28 us; the launch traced here: 27.8 us
  Pallas kernels  25.4 us (91%)
  local copies, waits for them, and re-layouts  2.38 us (8%)
    pallas_call x1, Pallas kernels, wide_blocks(): pl.pallas_call(functools.partial(exchange_kernel, n_seg, n_ch, group), ou...  22.8 us
    pallas_call x1, Pallas kernels, wide_blocks(): pl.pallas_call(functools.partial(lag_kernel, n_seg, half), out_shape=jax....  2.57 us
    unnamed x6, local copies, waits for them, and re-layouts  2.38 us

profile of v4, /device:TPU:0, one launch (start us, length us, event | category | flops | bytes accessed | tf_op | source)
XLA Modules:
  0.0 27.8 jit_solution(15772223308149625253)
XLA Ops:
  0.0 0.0 copy-start.2
  0.0 0.7 %copy-done.2 = s32[4]{0:T(128)S(1)} copy-done((s32[4]{0:T(128)S(1)}, s32[4]{0:T(128)}, u32[]{:S(2)}) %copy-start.2) | copy-done | bytes 40
  0.7 0.0 copy-start
  0.7 1.0 %copy-done = f32[1,64,2048]{2,1,0:T(8,128)S(1)} copy-done((f32[1,64,2048]{2,1,0:T(8,128)S(1)}, f32[1,64,2048]{2,1,0:T(8,128)}, u32[]{:S(2)}) %copy-start) | copy-done | bytes 524312
  1.7 0.0 copy-start.1
  1.7 0.7 %copy-done.1 = s32[4,16]{1,0:T(4,128)S(1)} copy-done((s32[4,16]{1,0:T(4,128)S(1)}, s32[4,16]{1,0:T(4,128)}, u32[]{:S(2)}) %copy-start.1) | copy-done | bytes 280
  2.4 22.8 %shard_map.37 = (bf16[2,1024,128]{2,1,0:T(8,128)(2,1)S(1)}, bf16[2,512,128]{2,1,0:T(8,128)(2,1)S(1)}) custom-call(f32[64,2048]{1,0:T(8,128)S(1)} %bitcast.2, s32[4]{0:T(128)S(1)} %copy-done.2, s32[4,16]{1,0:T(4,128)S(1)} %copy-done.1), custom_call_target="tpu_custom_call" | custom-call | tf_op jit(solution)/shard_map/pallas_call | solution.py:346
  25.2 2.6 %shard_map.38 = f32[32,64,128]{2,1,0:T(8,128)} custom-call(bf16[2,1024,128]{2,1,0:T(8,128)(2,1)S(1)} %get-tuple-element.7.d_ref, bf16[2,512,128]{2,1,0:T(8,128)(2,1)S(1)} %get-tuple-element.8.r_ref), custom_call_target="tpu_custom_call" | custom-call | tf_op jit(solution)/shard_map/pallas_call | solution.py:375
Async XLA Ops:
  0.0 0.7 %copy-start.2 = (s32[4]{0:T(128)S(1)}, s32[4]{0:T(128)}, u32[]{:S(2)}) copy-start(s32[4]{0:T(128)} %owners_hbm.1) | copy-start | bytes 52
  0.7 1.0 %copy-start = (f32[1,64,2048]{2,1,0:T(8,128)S(1)}, f32[1,64,2048]{2,1,0:T(8,128)}, u32[]{:S(2)}) copy-start(f32[1,64,2048]{2,1,0:T(8,128)} %param.3) | copy-start | bytes 1572868
  1.7 0.7 %copy-start.1 = (s32[4,16]{1,0:T(4,128)S(1)}, s32[4,16]{1,0:T(4,128)}, u32[]{:S(2)}) copy-start(s32[4,16]{1,0:T(4,128)} %local_hbm.1) | copy-start | bytes 772
